TPU v7x, 32 devices: a whole 2x2x4 slice. The times are simulated.
32 devices in a mesh: path: 2 (over x), mesh: 2 (over y), grid: 8 (over z, core).
Axes of the slice: x: 2, y: 2, z: 4, core: 2. Of those that a mesh axis runs over, the one named last changes fastest.
Arguments:
- path_bands: float32 [2, 16, 64, 64, 128], P('path', None, 'grid'), may hold values from -6 to 6
- occupied: float32 [2, 1, 64, 64, 128], P('mesh', None, 'grid', 'path'), may hold values from -6 to 6
- path_kpts: int32 [2, 3], P('path'), may hold values from 0 to 7
- mesh_kpts: int32 [2, 3], replicated, may hold values from 0 to 7
- mesh_shift: int32 [2, 3], replicated, may hold values from -1 to 1
Outputs:
- applied: float32 [2, 16, 64, 64, 128], P('path', 'mesh', 'grid')
- intersection: float32 [2, 2, 16, 16], P('path')
All inputs are finite; a program needn't handle non-finite values.
Results may differ from a plain program's by a relative error of at most 0.0001.
Values sent between devices are 32-bit elements; how exact they have to be, the bound alone decides.
No kernel may reach another device: no remote copies, remote signals or barrier semaphores. Data moves between devices by JAX's collectives and lax.ppermute only.
A program may use at most 64 MiB of HBM per device.

v0:
```python
import math
import jax
import jax.numpy as jnp
from jax import lax
from jax.sharding import PartitionSpec as P

KDIV = 8
BOX_LENGTH = 42.7
SCREEN_SQ = 0.04
MIXING = 0.25
HIGHEST_PRECISION = lax.Precision.HIGHEST


def signed_frequencies(indices, points):
    return (indices + points // 2) % points - points // 2


def dft_tables(positions, points):
    freqs = jnp.arange(points, dtype=jnp.int32)
    product = positions[:, None] * freqs[None, :] % points
    angles = 2.0 * math.pi / points * product.astype(jnp.float32)
    return (jnp.cos(angles), jnp.sin(angles))


def last_matrix(points, inverse):
    cosine_table, sine_table = dft_tables(jnp.arange(points, dtype=jnp.int32), points)
    if inverse:
        upper = jnp.concatenate([cosine_table, sine_table], 1)
        lower = jnp.concatenate([-sine_table, cosine_table], 1)
    else:
        upper = jnp.concatenate([cosine_table, -sine_table], 1)
        lower = jnp.concatenate([sine_table, cosine_table], 1)
    return jnp.concatenate([upper, lower], 0)


def along_axis(values, cosine_table, sine_table, contract_dim, inverse):
    letters = "abcde"
    form = (
        letters
        + ","
        + letters[contract_dim]
        + "w->"
        + letters[:contract_dim]
        + "w"
        + letters[contract_dim + 1 :]
    )
    cos_part = jnp.einsum(form, values, cosine_table, precision=HIGHEST_PRECISION)
    sin_part = jnp.einsum(form, values, sine_table, precision=HIGHEST_PRECISION)
    half_width = values.shape[-1] // 2
    sin_real = sin_part[..., :half_width]
    sin_imag = sin_part[..., half_width:]
    if inverse:
        return cos_part + jnp.concatenate([-sin_imag, sin_real], -1)
    return cos_part + jnp.concatenate([sin_imag, -sin_real], -1)


def rotate_orbitals(orbitals, shifts, x_planes):
    points = orbitals.shape[3]
    coords = jnp.arange(points, dtype=jnp.int32)
    product = (
        shifts[:, 0][:, None, None, None] * x_planes[None, :, None, None]
        + shifts[:, 1][:, None, None, None] * coords[None, None, :, None]
        + shifts[:, 2][:, None, None, None] * coords[None, None, None, :]
    ) % points
    angles = 2.0 * math.pi / points * product.astype(jnp.float32)
    cosines = jnp.cos(angles)[:, None]
    sines = jnp.sin(angles)[:, None]
    real_part = orbitals[..., :points]
    imag_part = orbitals[..., points:]
    return jnp.concatenate(
        [real_part * cosines - imag_part * sines, real_part * sines + imag_part * cosines], -1
    )


def pair_fields(rotated, band_fields):
    points = band_fields.shape[2]
    rot_real = rotated[..., :points][:, :, None]
    rot_imag = rotated[..., points:][:, :, None]
    band_real = band_fields[..., :points][None, None]
    band_imag = band_fields[..., points:][None, None]
    pairs = jnp.concatenate(
        [rot_real * band_real + rot_imag * band_imag, rot_real * band_imag - rot_imag * band_real],
        -1,
    )
    return pairs.reshape(
        (rotated.shape[0], rotated.shape[1] * band_fields.shape[0]) + band_fields.shape[1:]
    )


def accumulate(rotated, potential, nbands):
    points = rotated.shape[3]
    shaped = potential.reshape((rotated.shape[0], rotated.shape[1], nbands) + potential.shape[2:])
    rot_real = rotated[..., :points][:, :, None]
    rot_imag = rotated[..., points:][:, :, None]
    pot_real = shaped[..., :points]
    pot_imag = shaped[..., points:]
    summed = jnp.concatenate(
        [
            jnp.sum(rot_real * pot_real - rot_imag * pot_imag, axis=(0, 1)),
            jnp.sum(rot_real * pot_imag + rot_imag * pot_real, axis=(0, 1)),
        ],
        -1,
    )
    return -MIXING * summed


def intersection_part(band_fields, applied):
    points = band_fields.shape[2]
    nbands = band_fields.shape[0]
    band_real = band_fields[..., :points].reshape(nbands, -1)
    band_imag = band_fields[..., points:].reshape(nbands, -1)
    app_real = applied[..., :points].reshape(applied.shape[0], -1)
    app_imag = applied[..., points:].reshape(applied.shape[0], -1)
    real_sum = jnp.dot(band_real, app_real.T, precision=HIGHEST_PRECISION) + jnp.dot(
        band_imag, app_imag.T, precision=HIGHEST_PRECISION
    )
    imag_sum = jnp.dot(band_real, app_imag.T, precision=HIGHEST_PRECISION) - jnp.dot(
        band_imag, app_real.T, precision=HIGHEST_PRECISION
    )
    return jnp.stack([real_sum, imag_sum]) / float(points**3)


def screened_kernel(path_point, mesh_points, y_rows, points):
    offset_frac = (path_point[None, :] - mesh_points).astype(jnp.float32) / KDIV
    all_freqs = signed_frequencies(jnp.arange(points, dtype=jnp.int32), points).astype(jnp.float32)
    row_freqs = signed_frequencies(y_rows, points).astype(jnp.float32)
    square_x = (all_freqs[None, :] + offset_frac[:, 0:1]) ** 2
    square_y = (row_freqs[None, :] + offset_frac[:, 1:2]) ** 2
    square_z = (all_freqs[None, :] + offset_frac[:, 2:3]) ** 2
    squares = square_x[:, :, None, None] + square_y[:, None, :, None] + square_z[:, None, None, :]
    kernel = (
        4.0 * math.pi / ((2.0 * math.pi / BOX_LENGTH) ** 2 * squares + SCREEN_SQ) / float(points**3)
    )
    return jnp.concatenate([kernel, kernel], -1)


def per_device(path_bands, occupied, path_kpts, mesh_kpts, mesh_shift):
    points = path_bands.shape[3]
    nbands = path_bands.shape[1]
    local_planes = path_bands.shape[2]
    grid_count = lax.axis_size("grid")
    mesh_count = lax.axis_size("mesh")
    grid_index = lax.axis_index("grid")
    mesh_index = lax.axis_index("mesh")
    whole_orbitals = lax.all_gather(occupied, "path", axis=3, tiled=True)
    forward_z = last_matrix(points, False)
    inverse_z = last_matrix(points, True)
    cos_y, sin_y = dft_tables(jnp.arange(points, dtype=jnp.int32), points)
    band_all = path_bands[0]
    path_point = path_kpts[0]
    share_planes = local_planes // mesh_count
    both_orbitals = lax.all_to_all(whole_orbitals, "mesh", split_axis=2, concat_axis=0, tiled=True)
    x_planes = (
        grid_index * local_planes
        + mesh_index * share_planes
        + jnp.arange(share_planes, dtype=jnp.int32)
    )
    rotated = rotate_orbitals(both_orbitals, mesh_shift, x_planes)
    band_mine = lax.dynamic_slice_in_dim(band_all, mesh_index * share_planes, share_planes, 1)
    values = pair_fields(rotated, band_mine)
    values = jnp.matmul(values, forward_z, precision=HIGHEST_PRECISION)
    pair_field = along_axis(values, cos_y, sin_y, 3, False)
    wide_count = mesh_count * grid_count
    rows_y = points // wide_count
    flat_index = mesh_index * grid_count + grid_index
    y_rows = flat_index * rows_y + jnp.arange(rows_y, dtype=jnp.int32)
    kernel = screened_kernel(path_point, mesh_kpts, y_rows, points)
    positions = jnp.arange(points, dtype=jnp.int32)
    piece_index = positions // share_planes
    plane_index = (
        piece_index % grid_count * local_planes
        + piece_index // grid_count * share_planes
        + positions % share_planes
    )
    cos_x, sin_x = dft_tables(plane_index, points)
    moved = (
        along_axis(
            lax.all_to_all(pair_field, ("mesh", "grid"), split_axis=3, concat_axis=2, tiled=True),
            cos_x,
            sin_x,
            2,
            False,
        )
        * kernel[:, None]
    )
    moved = along_axis(moved, cos_x.T, sin_x.T, 2, True)
    potential = lax.all_to_all(moved, ("mesh", "grid"), split_axis=2, concat_axis=3, tiled=True)
    values = potential
    values = along_axis(values, cos_y, sin_y, 3, True)
    applied = accumulate(
        rotated, jnp.matmul(values, inverse_z, precision=HIGHEST_PRECISION), nbands
    )
    partial_value = intersection_part(band_mine, applied)
    result_bands = lax.all_to_all(applied, "mesh", split_axis=0, concat_axis=1, tiled=True)
    intersection = lax.psum(partial_value, ("mesh", "grid"))
    return (result_bands[None], intersection[None])


def solution(mesh):
    return jax.shard_map(
        per_device,
        mesh=mesh,
        in_specs=(
            P("path", None, "grid", None, None),
            P("mesh", None, "grid", "path", None),
            P("path", None),
            P(),
            P(),
        ),
        out_specs=(P("path", "mesh", "grid", None, None), P("path", None, None, None)),
        check_vma=False,
    )
```

profile of v0, /device:TPU:0, one launch (start us, length us, event | category | flops | bytes accessed | tf_op | source)
XLA Modules:
  0.0 395.5 jit_solution(9331506577557012715)
XLA Ops:
  0.6 9.0 %all_gather.3 = f32[1,1,8,64,128]{4,3,1,0,2:T(8,128)} all-gather(f32[1,1,8,32,128]{4,3,1,0,2:T(8,128)} %bitcast.138), channel_id=1, replica_groups=mesh['path'=2,'mesh'=2,'grid'=8] {'path'}, dimensions={3}, use_global_device_ids=true | all-gather | bytes 393216 | tf_op jit(solution)/shard_map/all_gather | solution.py:145
  9.6 3.4 all-to-all-start
  14.1 1.7 constant_dynamic-slice_fusion
  18.1 2.0 copy.20
  20.1 2.0 copy.21
  23.9 3.4 multiply_add_fusion
  27.3 4.0 %fusion = f32[2,16,4,64,128]{4,3,2,1,0:T(8,128)S(1)} fusion(f32[2,1,16,4,64,64]{5,4,3,2,0,1:T(8,128)S(1)} %get-tuple-element.11, f32[2,1,16,4,64,64]{5,4,3,2,0,1:T(8,128)S(1)} %get-tuple-element.10, f32[64,64]{1,0:T(8,128)S(1)} %get-tuple-element.29, f32[64,64]{1,0:T(8,128)S(1)} %get-tuple-element.28, f32[64,64]{1,0:T(8,128)S(1)} %fusion.88), kind=kOutput, calls=%fused_computation.5 | convolution fusion | flops 1611710464 | bytes 8437760 | tf_op jit(solution)/shard_map/dot_general | solution.py:161
  31.3 4.2 %convolution_bitcast_fusion.3 = f32[2,16,4,64,128]{4,3,2,1,0:T(8,128)S(1)} fusion(f32[2,16,4,64,128]{4,3,2,1,0:T(8,128)S(1)} %fusion), kind=kOutput, calls=%fused_computation.25 | convolution fusion | flops 805363712 | bytes 8388608 | tf_op jit(solution)/shard_map/abcde,dw->abcwe/dot_general | solution.py:48
  35.5 1.9 fusion.139
  37.4 19.3 %maximum_add_fusion = f32[2,16,4,64,128]{4,3,2,1,0:T(8,128)S(1)} fusion(f32[2,16,4,64,64]{4,3,2,1,0:T(8,128)S(1)} %get-tuple-element.19, f32[2,16,4,64,64]{4,3,2,1,0:T(8,128)S(1)} %get-tuple-element.18, f32[2,16,4,64,128]{4,3,2,1,0:T(8,128)S(1)} %fusion), kind=kOutput, calls=%fused_computation.8 | convolution fusion | flops 807460864 | bytes 12582912 | tf_op jit(solution)/shard_map/abcde,dw->abcwe/dot_general | solution.py:47
  56.6 4.7 %copy.24 = f32[2,16,4,64,128]{4,2,1,0,3:T(4,128)} copy(f32[2,16,4,64,128]{4,3,2,1,0:T(8,128)S(1)} %maximum_add_fusion) | data formatting | bytes 8388608 | tf_op jit(solution)/shard_map/add | solution.py:54
  61.3 6.6 %all-to-all-start.1 = ((f32[2,16,4,64,128]{4,2,1,0,3:T(4,128)}), f32[2,16,4,64,128]{4,2,1,0,3:T(4,128)}, u32[]{:S(2)}, u32[]{:S(2)}) async-start(f32[2,16,4,64,128]{4,2,1,0,3:T(4,128)} %copy.24), calls=%async_computation.1 | async-start | bytes 8388608 | tf_op jit(solution)/shard_map/all_to_all | solution.py:178
  68.7 87.0 %all-to-all-done.1 = f32[2,16,4,64,128]{4,2,1,0,3:T(4,128)} async-done(((f32[2,16,4,64,128]{4,2,1,0,3:T(4,128)}), f32[2,16,4,64,128]{4,2,1,0,3:T(4,128)}, u32[]{:S(2)}, u32[]{:S(2)}) %all-to-all-start.1) | async-done | bytes 4194336 | tf_op jit(solution)/shard_map/all_to_all | solution.py:178
  155.7 3.4 copy.25
  159.1 4.2 %convolution_bitcast_fusion.2 = f32[2,16,64,4,128]{4,2,3,1,0:T(8,128)S(1)} fusion(f32[2,16,64,4,128]{4,2,3,1,0:T(8,128)S(1)} %bitcast.131, s32[64]{0:T(128)S(1)} %fusion.91), kind=kOutput, calls=%fused_computation.24 | convolution fusion | flops 805363712 | bytes 8388864 | tf_op jit(solution)/shard_map/abcde,cw->abwde/dot_general | solution.py:48
  163.3 1.9 fusion.138
  165.2 6.8 %fusion.3 = f32[2,16,64,4,128]{4,2,3,1,0:T(8,128)S(1)} fusion(f32[2,16,64,4,64]{4,2,3,1,0:T(8,128)S(1)} %get-tuple-element.17, f32[2,16,64,4,64]{4,2,3,1,0:T(8,128)S(1)} %get-tuple-element.16, f32[2,16,64,4,128]{4,2,3,1,0:T(8,128)S(1)} %bitcast.132, f32[2,64,4,128]{3,1,2,0:T(8,128)S(1)} %pad_maximum_fusion, s32[64]{0:T(128)S(1)} %fusion.91), kind=kOutput, calls=%fused_computation.10 | convolution fusion | flops 808509440 | bytes 12845312 | tf_op jit(solution)/shard_map/abcde,cw->abwde/dot_general | solution.py:47
  172.0 4.3 %convolution_bitcast_fusion.1 = f32[2,16,64,4,128]{4,2,3,1,0:T(8,128)S(1)} fusion(f32[2,16,64,4,128]{4,2,3,1,0:T(8,128)S(1)} %fusion.3, s32[64]{0:T(128)S(1)} %fusion.91), kind=kOutput, calls=%fused_computation.23 | convolution fusion | flops 805363712 | bytes 8388864 | tf_op jit(solution)/shard_map/abcde,cw->abwde/dot_general | solution.py:48
  178.0 6.3 %maximum_add_fusion.2 = f32[2,16,64,4,128]{4,2,3,1,0:T(8,128)S(1)} fusion(f32[2,16,64,4,64]{4,2,3,1,0:T(8,128)S(1)} %get-tuple-element.15, f32[2,16,64,4,64]{4,2,3,1,0:T(8,128)S(1)} %get-tuple-element.14, f32[2,16,64,4,128]{4,2,3,1,0:T(8,128)S(1)} %fusion.3, s32[64]{0:T(128)S(1)} %fusion.91), kind=kOutput, calls=%fused_computation.11 | convolution fusion | flops 807460864 | bytes 12583168 | tf_op jit(solution)/shard_map/abcde,cw->abwde/dot_general | solution.py:47
  184.3 2.9 copy.28
  187.2 101.4 %all_to_all.63 = f32[2,16,64,4,128]{4,3,1,0,2:T(4,128)S(1)} all-to-all(f32[2,16,64,4,128]{4,3,1,0,2:T(4,128)S(1)} %copy.28), channel_id=1, replica_groups=mesh['path'=2,'mesh'=2,'grid'=8] {'mesh','grid'}, dimensions={2} | all-to-all | bytes 8388608 | tf_op jit(solution)/shard_map/all_to_all | solution.py:187
  289.8 4.2 %convolution_bitcast_fusion = f32[2,16,4,64,128]{4,3,2,1,0:T(8,128)S(1)} fusion(f32[2,16,4,64,128]{4,3,2,1,0:T(8,128)S(1)} %bitcast.133), kind=kOutput, calls=%fused_computation.22 | convolution fusion | flops 805363712 | bytes 8388608 | tf_op jit(solution)/shard_map/abcde,dw->abcwe/dot_general | solution.py:48
  294.0 4.2 %fusion.65 = f32[64,2,16,4,128]{4,0,3,2,1:T(8,128)S(1)} fusion(f32[2,16,4,64,128]{4,3,2,1,0:T(8,128)S(1)} %bitcast.134), kind=kOutput, calls=%fused_computation.85 | convolution fusion | flops 805363712 | bytes 8388608 | tf_op jit(solution)/shard_map/abcde,dw->abcwe/dot_general | solution.py:47
  299.9 4.2 %fusion.8 = f32[2,1,16,4,64,128]{5,4,3,2,0,1:T(8,128)S(1)} fusion(f32[2,16,4,64,64]{4,3,2,1,0:T(8,128)S(1)} %get-tuple-element.13, f32[2,16,4,64,64]{4,3,2,1,0:T(8,128)S(1)} %get-tuple-element.12, f32[64,2,16,4,128]{4,0,3,2,1:T(8,128)S(1)} %fusion.65, f32[64,64]{1,0:T(8,128)S(1)} %get-tuple-element.29, f32[64,64]{1,0:T(8,128)S(1)} %fusion.88, ...), kind=kOutput, calls=%fused_computation.21 | convolution fusion | flops 1612759040 | bytes 12632064 | tf_op jit(solution)/shard_map/dot_general | solution.py:191
  309.9 2.0 copy.33
  311.9 5.1 %all-to-all-start.3 = ((f32[16,4,64,128]{3,2,1,0:T(8,128)}), f32[16,4,64,128]{3,2,1,0:T(8,128)}, u32[]{:S(2)}, u32[]{:S(2)}) async-start(f32[16,4,64,128]{3,2,1,0:T(8,128)} %copy.33), calls=%async_computation.3 | async-start | bytes 4194304 | tf_op jit(solution)/shard_map/all_to_all | solution.py:194
  317.0 4.6 %fusion.17 = f32[16,16]{1,0:T(8,128)S(1)} fusion(f32[16,4,64,128]{3,0,2,1:T(8,128)} %copy-done, f32[16,4,64,128]{3,0,2,1:T(8,128)S(1)} %bitcast.127), kind=kOutput, calls=%fused_computation.36 | convolution fusion | flops 50331648 | bytes 4195328 | tf_op jit(solution)/shard_map/dot_general | solution.py:114
  321.6 2.9 fusion.20
  324.5 3.3 fusion.38
  327.7 2.9 fusion.32
  330.7 61.4 %psum.7 = f32[1,2,16,16]{3,2,1,0:T(8,128)} all-reduce(f32[1,2,16,16]{3,2,1,0:T(8,128)S(1)} %fusion.77), channel_id=1, replica_groups=mesh['path'=2,'mesh'=2,'grid'=8] {'mesh','grid'}, use_global_device_ids=true, to_apply=%region_2.3 | all-reduce | flops 512 | bytes 4096 | tf_op jit(solution)/shard_map/psum | solution.py:195
  392.1 3.2 copy.34
  (38 shorter events, 16.1 us)
Async XLA Ops:
  9.6 12.6 %all-to-all-start = ((f32[1,1,8,64,128]{4,3,1,0,2:T(8,128)}), f32[1,1,8,64,128]{4,3,1,0,2:T(8,128)S(1)}, u32[]{:S(2)}, u32[]{:S(2)}) async-start(f32[1,1,8,64,128]{4,3,1,0,2:T(8,128)} %all_gather.3), calls=%async_computation | async-start | bytes 524288 | tf_op jit(solution)/shard_map/all_to_all | solution.py:152
  61.3 6.7 %copy-start.2 = (s32[2,3]{1,0:T(2,128)S(1)}, s32[2,3]{1,0:T(2,128)}, u32[]{:S(2)}) copy-start(s32[2,3]{1,0:T(2,128)} %param.8) | copy-start | bytes 76
  61.3 6.7 %copy-start.3 = (s32[1,3]{1,0:T(1,128)S(1)}, s32[1,3]{1,0:T(1,128)}, u32[]{:S(2)}) copy-start(s32[1,3]{1,0:T(1,128)} %param.7) | copy-start | bytes 40
  61.3 94.4 %all-to-all-start.1 = ((f32[2,16,4,64,128]{4,2,1,0,3:T(4,128)}), f32[2,16,4,64,128]{4,2,1,0,3:T(4,128)}, u32[]{:S(2)}, u32[]{:S(2)}) async-start(f32[2,16,4,64,128]{4,2,1,0,3:T(4,128)} %copy.24), calls=%async_computation.1 | async-start | bytes 8388608 | tf_op jit(solution)/shard_map/all_to_all | solution.py:178
  308.6 1.3 copy-start
  311.9 80.2 %all-to-all-start.3 = ((f32[16,4,64,128]{3,2,1,0:T(8,128)}), f32[16,4,64,128]{3,2,1,0:T(8,128)}, u32[]{:S(2)}, u32[]{:S(2)}) async-start(f32[16,4,64,128]{3,2,1,0:T(8,128)} %copy.33), calls=%async_computation.3 | async-start | bytes 4194304 | tf_op jit(solution)/shard_map/all_to_all | solution.py:194
  317.0 4.6 %copy-start.1 = (f32[16,4,64,128]{3,0,2,1:T(8,128)S(1)}, f32[16,4,64,128]{3,0,2,1:T(8,128)}, u32[]{:S(2)}) copy-start(f32[16,4,64,128]{3,0,2,1:T(8,128)} %copy-done) | copy-start | bytes 6291460
where the time goes:
time: 400 us; the launch traced here: 396 us
  blocking collectives  172 us (43%)
  waiting for transfers between devices  87 us (22%)
  matrix products  75.3 us (19%)
  local copies, waits for them, and re-layouts  29.8 us (7%)
  other arithmetic  15.3 us (4%)
  starting transfers between devices  15.1 us (4%)
    all_to_all x1, blocking collectives, per_device(): lax.all_to_all(moved, ('mesh', 'grid'), split_axis=2, concat_axis=3, tile...  101 us
    all_to_all x1, waiting for transfers between devices, per_device(): lax.all_to_all(pair_field, ('mesh', 'grid'), split_axis=3, concat_axis=2,...  87 us
    psum x1, blocking collectives, per_device(): intersection = lax.psum(partial_value, ('mesh', 'grid'))  61.4 us
    dot_general x4, matrix products, along_axis(): jnp.einsum(form, values, cosine_table, precision=HIGHEST_PRECISION)  36.5 us
    dot_general x4, matrix products, along_axis(): sin_part = jnp.einsum(form, values, sine_table, precision=HIGHEST_PRECISION)  16.9 us
    all_gather x1, blocking collectives, per_device(): whole_orbitals = lax.all_gather(occupied, 'path', axis=3, tiled=True)  8.98 us
  transfers between devices with their start and end apart: 3, of which 1 were waited for; matrix products, arithmetic and copies ran while one was open for 6% of the time, Pallas kernels for 0%

commit v1 on v0

--- a/solution.py
+++ b/solution.py
@@ -184,7 +184,9 @@
         * kernel[:, None]
     )
     moved = along_axis(moved, cos_x.T, sin_x.T, 2, True)
-    potential = lax.all_to_all(moved, ("mesh", "grid"), split_axis=2, concat_axis=3, tiled=True)
+    shards = jnp.split(moved, lax.axis_size(("mesh", "grid")), axis=2)
+    received = lax.all_to_all(jnp.stack(shards), ("mesh", "grid"), 0, 0)
+    potential = jnp.concatenate(received, axis=3)
     values = potential
     values = along_axis(values, cos_y, sin_y, 3, True)
     applied = accumulate(

time: 400 us -> 402 us (level)
  no operation moved by 1% of the time
where the time goes in v1:
time: 402 us; the launch traced here: 397 us
  blocking collectives  172 us (43%)
  waiting for transfers between devices  87 us (22%)
  matrix products  77.9 us (19%)
  local copies, waits for them, and re-layouts  28.4 us (7%)
  other arithmetic  15.5 us (4%)
  starting transfers between devices  15.1 us (4%)
    all_to_all x1, blocking collectives, per_device(): received = lax.all_to_all(jnp.stack(shards), ('mesh', 'grid'), 0, 0)  101 us
    all_to_all x1, waiting for transfers between devices, per_device(): lax.all_to_all(pair_field, ('mesh', 'grid'), split_axis=3, concat_axis=2,...  87 us
    psum x1, blocking collectives, per_device(): intersection = lax.psum(partial_value, ('mesh', 'grid'))  61.4 us
    dot_general x4, matrix products, along_axis(): jnp.einsum(form, values, cosine_table, precision=HIGHEST_PRECISION)  37.9 us
    dot_general x4, matrix products, along_axis(): sin_part = jnp.einsum(form, values, sine_table, precision=HIGHEST_PRECISION)  18.4 us
    all_gather x1, blocking collectives, per_device(): whole_orbitals = lax.all_gather(occupied, 'path', axis=3, tiled=True)  8.98 us
  transfers between devices with their start and end apart: 3, of which 1 were waited for; matrix products, arithmetic and copies ran while one was open for 6% of the time, Pallas kernels for 0%

profile of v1, /device:TPU:0, one launch (start us, length us, event | category | flops | bytes accessed | tf_op | source)
XLA Modules:
  0.0 397.3 jit_solution(11691640065967811814)
XLA Ops:
  0.6 9.0 %all_gather.3 = f32[1,1,8,64,128]{4,3,1,0,2:T(8,128)} all-gather(f32[1,1,8,32,128]{4,3,1,0,2:T(8,128)} %bitcast.196), channel_id=1, replica_groups=mesh['path'=2,'mesh'=2,'grid'=8] {'path'}, dimensions={3}, use_global_device_ids=true | all-gather | bytes 393216 | tf_op jit(solution)/shard_map/all_gather | solution.py:145
  9.6 3.4 all-to-all-start
  14.1 1.7 constant_dynamic-slice_fusion
  18.1 2.0 copy.31
  20.1 2.0 copy.32
  23.9 3.4 multiply_add_fusion
  27.3 4.0 %fusion = f32[2,16,4,64,128]{4,3,2,1,0:T(8,128)S(1)} fusion(f32[2,1,16,4,64,64]{5,4,3,2,0,1:T(8,128)S(1)} %get-tuple-element.11, f32[2,1,16,4,64,64]{5,4,3,2,0,1:T(8,128)S(1)} %get-tuple-element.10, f32[64,64]{1,0:T(8,128)S(1)} %get-tuple-element.29, f32[64,64]{1,0:T(8,128)S(1)} %get-tuple-element.28, f32[64,64]{1,0:T(8,128)S(1)} %fusion.110), kind=kOutput, calls=%fused_computation.5 | convolution fusion | flops 1611710464 | bytes 8437760 | tf_op jit(solution)/shard_map/dot_general | solution.py:161
  31.3 4.2 %convolution_bitcast_fusion.2 = f32[2,16,4,64,128]{4,3,2,1,0:T(8,128)S(1)} fusion(f32[2,16,4,64,128]{4,3,2,1,0:T(8,128)S(1)} %fusion), kind=kOutput, calls=%fused_computation.29 | convolution fusion | flops 805363712 | bytes 8388608 | tf_op jit(solution)/shard_map/abcde,dw->abcwe/dot_general | solution.py:48
  35.5 1.9 fusion.161
  37.4 19.3 %maximum_add_fusion = f32[2,16,4,64,128]{4,3,2,1,0:T(8,128)S(1)} fusion(f32[2,16,4,64,64]{4,3,2,1,0:T(8,128)S(1)} %get-tuple-element.19, f32[2,16,4,64,64]{4,3,2,1,0:T(8,128)S(1)} %get-tuple-element.18, f32[2,16,4,64,128]{4,3,2,1,0:T(8,128)S(1)} %fusion), kind=kOutput, calls=%fused_computation.8 | convolution fusion | flops 807460864 | bytes 12582912 | tf_op jit(solution)/shard_map/abcde,dw->abcwe/dot_general | solution.py:47
  56.6 4.7 %copy.35 = f32[2,16,4,64,128]{4,2,1,0,3:T(4,128)} copy(f32[2,16,4,64,128]{4,3,2,1,0:T(8,128)S(1)} %maximum_add_fusion) | data formatting | bytes 8388608 | tf_op jit(solution)/shard_map/add | solution.py:54
  61.3 6.6 %all-to-all-start.1 = ((f32[2,16,4,64,128]{4,2,1,0,3:T(4,128)}), f32[2,16,4,64,128]{4,2,1,0,3:T(4,128)}, u32[]{:S(2)}, u32[]{:S(2)}) async-start(f32[2,16,4,64,128]{4,2,1,0,3:T(4,128)} %copy.35), calls=%async_computation.1 | async-start | bytes 8388608 | tf_op jit(solution)/shard_map/all_to_all | solution.py:178
  68.7 87.0 %all-to-all-done.1 = f32[2,16,4,64,128]{4,2,1,0,3:T(4,128)} async-done(((f32[2,16,4,64,128]{4,2,1,0,3:T(4,128)}), f32[2,16,4,64,128]{4,2,1,0,3:T(4,128)}, u32[]{:S(2)}, u32[]{:S(2)}) %all-to-all-start.1) | async-done | bytes 4194336 | tf_op jit(solution)/shard_map/all_to_all | solution.py:178
  155.7 3.4 copy.36
  159.1 4.2 %convolution_bitcast_fusion.1 = f32[2,16,64,4,128]{4,2,3,1,0:T(8,128)S(1)} fusion(f32[2,16,64,4,128]{4,2,3,1,0:T(8,128)S(1)} %bitcast.189, s32[64]{0:T(128)S(1)} %fusion.113), kind=kOutput, calls=%fused_computation.28 | convolution fusion | flops 805363712 | bytes 8388864 | tf_op jit(solution)/shard_map/abcde,cw->abwde/dot_general | solution.py:48
  163.3 1.9 fusion.160
  165.2 6.8 %fusion.3 = f32[2,16,64,4,128]{4,2,3,1,0:T(8,128)S(1)} fusion(f32[2,16,64,4,64]{4,2,3,1,0:T(8,128)S(1)} %get-tuple-element.17, f32[2,16,64,4,64]{4,2,3,1,0:T(8,128)S(1)} %get-tuple-element.16, f32[2,16,64,4,128]{4,2,3,1,0:T(8,128)S(1)} %bitcast.190, f32[2,64,4,128]{3,1,2,0:T(8,128)S(1)} %pad_maximum_fusion, s32[64]{0:T(128)S(1)} %fusion.113), kind=kOutput, calls=%fused_computation.10 | convolution fusion | flops 808509440 | bytes 12845312 | tf_op jit(solution)/shard_map/abcde,cw->abwde/dot_general | solution.py:47
  172.0 4.3 %convolution_bitcast_fusion = f32[2,16,64,4,128]{4,2,3,1,0:T(8,128)S(1)} fusion(f32[2,16,64,4,128]{4,2,3,1,0:T(8,128)S(1)} %fusion.3, s32[64]{0:T(128)S(1)} %fusion.113), kind=kOutput, calls=%fused_computation.27 | convolution fusion | flops 805363712 | bytes 8388864 | tf_op jit(solution)/shard_map/abcde,cw->abwde/dot_general | solution.py:48
  178.0 6.2 %maximum_add_fusion.2 = f32[2,16,64,4,128]{4,2,3,1,0:T(8,128)S(1)} fusion(f32[2,16,64,4,64]{4,2,3,1,0:T(8,128)S(1)} %get-tuple-element.15, f32[2,16,64,4,64]{4,2,3,1,0:T(8,128)S(1)} %get-tuple-element.14, f32[2,16,64,4,128]{4,2,3,1,0:T(8,128)S(1)} %fusion.3, s32[64]{0:T(128)S(1)} %fusion.113), kind=kOutput, calls=%fused_computation.11 | convolution fusion | flops 807460864 | bytes 12583168 | tf_op jit(solution)/shard_map/abcde,cw->abwde/dot_general | solution.py:47
  185.7 101.4 %all_to_all.50 = f32[16,2,16,4,4,128]{5,3,4,2,1,0:T(4,128)S(1)} all-to-all(f32[16,2,16,4,4,128]{5,3,4,2,1,0:T(4,128)S(1)} %fusion.51), channel_id=1, replica_groups=mesh['path'=2,'mesh'=2,'grid'=8] {'mesh','grid'}, dimensions={0} | all-to-all | bytes 8388608 | tf_op jit(solution)/shard_map/all_to_all | solution.py:188
  288.4 5.7 %fusion.12 = f32[2,16,4,64,128]{4,3,2,1,0:T(8,128)S(1)} fusion(f32[2,16,4,64,128]{4,1,3,2,0:T(8,128)S(1)} %bitcast.191), kind=kOutput, calls=%fused_computation.25 | convolution fusion | flops 805363712 | bytes 8388608 | tf_op jit(solution)/shard_map/abcde,dw->abcwe/dot_general | solution.py:48
  294.1 5.7 %fusion.10 = f32[64,2,16,4,128]{4,0,3,2,1:T(8,128)S(1)} fusion(f32[2,16,4,64,128]{4,1,3,2,0:T(8,128)S(1)} %bitcast.192), kind=kOutput, calls=%fused_computation.23 | convolution fusion | flops 805363712 | bytes 8388608 | tf_op jit(solution)/shard_map/abcde,dw->abcwe/dot_general | solution.py:47
  299.8 1.9 slice_negate_fusion
  301.7 4.0 %fusion.15 = f32[2,1,16,4,64,128]{5,4,3,2,0,1:T(8,128)S(1)} fusion(f32[2,16,4,64,64]{4,3,2,1,0:T(8,128)S(1)} %get-tuple-element.13, f32[2,16,4,64,64]{4,3,2,1,0:T(8,128)S(1)} %get-tuple-element.12, f32[64,2,16,4,128]{4,0,3,2,1:T(8,128)S(1)} %fusion.10, f32[64,64]{1,0:T(8,128)S(1)} %get-tuple-element.29, f32[64,64]{1,0:T(8,128)S(1)} %fusion.110, ...), kind=kOutput, calls=%fused_computation.26 | convolution fusion | flops 1612759040 | bytes 12632064 | tf_op jit(solution)/shard_map/dot_general | solution.py:193
  311.5 2.0 copy.46
  313.5 5.1 %all-to-all-start.3 = ((f32[16,4,64,128]{3,2,1,0:T(8,128)}), f32[16,4,64,128]{3,2,1,0:T(8,128)}, u32[]{:S(2)}, u32[]{:S(2)}) async-start(f32[16,4,64,128]{3,2,1,0:T(8,128)} %copy.46), calls=%async_computation.3 | async-start | bytes 4194304 | tf_op jit(solution)/shard_map/all_to_all | solution.py:196
  318.6 4.6 %fusion.24 = f32[16,16]{1,0:T(8,128)S(1)} fusion(f32[16,4,64,128]{3,0,2,1:T(8,128)} %copy-done, f32[16,4,64,128]{3,0,2,1:T(8,128)S(1)} %bitcast.185), kind=kOutput, calls=%fused_computation.40 | convolution fusion | flops 50331648 | bytes 4195328 | tf_op jit(solution)/shard_map/dot_general | solution.py:114
  323.2 2.9 fusion.27
  326.0 3.3 fusion.45
  329.3 2.9 fusion.39
  332.2 61.4 %psum.7 = f32[1,2,16,16]{3,2,1,0:T(8,128)} all-reduce(f32[1,2,16,16]{3,2,1,0:T(8,128)S(1)} %fusion.99), channel_id=1, replica_groups=mesh['path'=2,'mesh'=2,'grid'=8] {'mesh','grid'}, use_global_device_ids=true, to_apply=%region_2.3 | all-reduce | flops 512 | bytes 4096 | tf_op jit(solution)/shard_map/psum | solution.py:197
  393.7 3.2 copy.47
  (53 shorter events, 15.9 us)
Async XLA Ops:
  9.6 12.6 %all-to-all-start = ((f32[1,1,8,64,128]{4,3,1,0,2:T(8,128)}), f32[1,1,8,64,128]{4,3,1,0,2:T(8,128)S(1)}, u32[]{:S(2)}, u32[]{:S(2)}) async-start(f32[1,1,8,64,128]{4,3,1,0,2:T(8,128)} %all_gather.3), calls=%async_computation | async-start | bytes 524288 | tf_op jit(solution)/shard_map/all_to_all | solution.py:152
  61.3 6.7 %copy-start.2 = (s32[2,3]{1,0:T(2,128)S(1)}, s32[2,3]{1,0:T(2,128)}, u32[]{:S(2)}) copy-start(s32[2,3]{1,0:T(2,128)} %param.8) | copy-start | bytes 76
  61.3 6.7 %copy-start.3 = (s32[1,3]{1,0:T(1,128)S(1)}, s32[1,3]{1,0:T(1,128)}, u32[]{:S(2)}) copy-start(s32[1,3]{1,0:T(1,128)} %param.7) | copy-start | bytes 40
  61.3 94.4 %all-to-all-start.1 = ((f32[2,16,4,64,128]{4,2,1,0,3:T(4,128)}), f32[2,16,4,64,128]{4,2,1,0,3:T(4,128)}, u32[]{:S(2)}, u32[]{:S(2)}) async-start(f32[2,16,4,64,128]{4,2,1,0,3:T(4,128)} %copy.35), calls=%async_computation.1 | async-start | bytes 8388608 | tf_op jit(solution)/shard_map/all_to_all | solution.py:178
  310.2 1.3 copy-start
  313.5 80.2 %all-to-all-start.3 = ((f32[16,4,64,128]{3,2,1,0:T(8,128)}), f32[16,4,64,128]{3,2,1,0:T(8,128)}, u32[]{:S(2)}, u32[]{:S(2)}) async-start(f32[16,4,64,128]{3,2,1,0:T(8,128)} %copy.46), calls=%async_computation.3 | async-start | bytes 4194304 | tf_op jit(solution)/shard_map/all_to_all | solution.py:196
  318.5 4.6 %copy-start.1 = (f32[16,4,64,128]{3,0,2,1:T(8,128)S(1)}, f32[16,4,64,128]{3,0,2,1:T(8,128)}, u32[]{:S(2)}) copy-start(f32[16,4,64,128]{3,0,2,1:T(8,128)} %copy-done) | copy-start | bytes 6291460
